TPU v7x, 32 devices: a whole 2x2x4 slice. The times are simulated.
32 devices in a mesh: dp: 16 (over z, y, core), tensor: 2 (over x).
Axes of the slice: x: 2, y: 2, z: 4, core: 2. Of those that a mesh axis runs over, the one named last changes fastest.
Arguments:
- layer_input: float32 [8192, 1024], P(('dp', 'tensor')), may hold values from -6 to 6
- segment_ids: int32 [16, 512], P('dp'), may hold values from 0 to 3, never falling along the last dimension, each value on 1 to 256 neighbouring positions
- norm1_gain: bfloat16 [1024], P('dp'), may hold values from 0.25 to 1.75
- norm1_shift: bfloat16 [1024], P('dp'), may hold values from -3 to 3
- qkv_weight: bfloat16 [1024, 3072], P('dp', 'tensor'), may hold values from -1 to 1
- qkv_bias: bfloat16 [2048], P(('tensor', 'dp')), may hold values from -3 to 3
- dense_weight: bfloat16 [1024, 1024], P('dp', 'tensor'), may hold values from -0.75 to 0.75
- dense_bias: bfloat16 [1024], P('dp'), may hold values from -3 to 3
- norm2_gain: bfloat16 [1024], P('dp'), may hold values from 0.25 to 1.75
- norm2_shift: bfloat16 [1024], P('dp'), may hold values from -3 to 3
- inner_weight: bfloat16 [1024, 4096], P('dp', 'tensor'), may hold values from -0.1875 to 0.1875
- inner_bias: bfloat16 [4096], P(('tensor', 'dp')), may hold values from -3 to 3
- outer_weight: bfloat16 [1024, 4096], P('dp', 'tensor'), may hold values from -0.1875 to 0.1875
- outer_bias: bfloat16 [1024], P('dp'), may hold values from -3 to 3
- out_cotangent: float32 [8192, 1024], P(('dp', 'tensor')), may hold values from -6 to 6
Outputs:
- layer_output: float32 [8192, 1024], P(('dp', 'tensor'))
- input_grad: float32 [8192, 1024], P(('dp', 'tensor'))
- norm1_gain_grad: float32 [1024], P('dp')
- norm1_shift_grad: float32 [1024], P('dp')
- qkv_weight_grad: float32 [1024, 3072], P('dp', 'tensor')
- qkv_bias_grad: float32 [2048], P(('tensor', 'dp'))
- dense_weight_grad: float32 [1024, 1024], P('dp', 'tensor')
- dense_bias_grad: float32 [1024], P('dp')
- norm2_gain_grad: float32 [1024], P('dp')
- norm2_shift_grad: float32 [1024], P('dp')
- inner_weight_grad: float32 [1024, 4096], P('dp', 'tensor')
- inner_bias_grad: float32 [4096], P(('tensor', 'dp'))
- outer_weight_grad: float32 [1024, 4096], P('dp', 'tensor')
- outer_bias_grad: float32 [1024], P('dp')
Inputs may be any that keep to these rules, and one draw needn't show every extreme that they name: `segment_ids`: along each row the ids never fall; each segment spans 1 to 256 positions, and one spans exactly 256.
All inputs are finite; a program needn't handle non-finite values.
Results may differ from a plain program's by a relative error of at most 0.024.
Values may be sent and summed in bfloat16 or wider, within the bound.
No kernel may reach another device: no remote copies, remote signals or barrier semaphores. Data moves between devices by JAX's collectives and lax.ppermute only.
A program may use at most 128 MiB of HBM per device.

v0:
```python
import jax
import jax.numpy as jnp
from jax import lax
from jax.sharding import PartitionSpec as P

H = 16
HD = 64
EPSILON = 1e-05
GELU_C = 0.7978845608028654
GELU_K = 0.044715


def layer_norm(row_data, gain, shift):
    row_mean = jnp.mean(row_data, axis=-1, keepdims=True)
    centered = row_data - row_mean
    row_var = jnp.mean(centered * centered, axis=-1, keepdims=True)
    inv_std = lax.rsqrt(row_var + EPSILON)
    normed = centered * inv_std
    return (normed * gain.astype(jnp.float32) + shift.astype(jnp.float32), normed, inv_std)


def norm_back(grad_out, normed, inv_std, gain):
    scaled = grad_out * gain.astype(jnp.float32)
    mean_grad = jnp.mean(scaled, axis=-1, keepdims=True)
    mean_cross = jnp.mean(scaled * normed, axis=-1, keepdims=True)
    return inv_std * (scaled - mean_grad - normed * mean_cross)


def gelu_parts(pre_act):
    cubed_term = pre_act * pre_act * pre_act
    tangent = jnp.tanh(GELU_C * (pre_act + GELU_K * cubed_term))
    result = 0.5 * pre_act * (1.0 + tangent)
    derivative = 0.5 * (1.0 + tangent) + 0.5 * pre_act * (1.0 - tangent * tangent) * GELU_C * (
        1.0 + 3.0 * GELU_K * pre_act * pre_act
    )
    return (result, derivative)


def rows_product(left, right):
    return lax.dot_general(
        left, right, (((0,), (0,)), ((), ())), preferred_element_type=jnp.float32
    )


def cross_product(left, right):
    return lax.dot_general(
        left, right, (((1,), (1,)), ((), ())), preferred_element_type=jnp.float32
    )


def block_scores(query_block, key_rows, segment_row, head_slopes):
    block_len = query_block.shape[0]
    scores = jnp.einsum(
        "bhe,the->hbt", query_block, key_rows, preferred_element_type=jnp.float32
    ) * HD ** (-0.5)
    row_pos = jnp.arange(block_len, dtype=jnp.int32)
    col_pos = jnp.arange(key_rows.shape[0], dtype=jnp.int32)
    allowed = (col_pos[None, :] <= row_pos[:, None]) & (
        segment_row[:, None] == segment_row[None, :]
    )
    distance = (row_pos[:, None] - col_pos[None, :]).astype(jnp.float32)
    scores = scores - head_slopes[:, None, None] * distance[None]
    return jnp.where(allowed[None], scores, -1e30)


def attend_forward(query_rows, key_rows, value_rows, segment_row, head_slopes):
    scores = block_scores(query_rows, key_rows, segment_row, head_slopes)
    row_max = jnp.max(scores, axis=-1, keepdims=True)
    log_total = row_max + jnp.log(jnp.sum(jnp.exp(scores - row_max), axis=-1, keepdims=True))
    attn_probs = jnp.exp(scores - log_total).astype(jnp.bfloat16)
    context = jnp.einsum("hbt,the->bhe", attn_probs, value_rows, preferred_element_type=jnp.float32)
    outputs = context.astype(jnp.bfloat16)
    return (outputs, log_total)


def attend_backward(
    query_rows, key_rows, value_rows, context, context_grad, log_total, segment_row, head_slopes
):
    scale = HD ** (-0.5)
    scores = block_scores(query_rows, key_rows, segment_row, head_slopes)
    probs = jnp.exp(scores - log_total)
    probs_low = probs.astype(jnp.bfloat16)
    value_grad = jnp.einsum(
        "hbt,bhe->the", probs_low, context_grad, preferred_element_type=jnp.float32
    )
    prob_grad = jnp.einsum(
        "bhe,the->hbt", context_grad, value_rows, preferred_element_type=jnp.float32
    )
    delta = jnp.sum(context_grad.astype(jnp.float32) * context.astype(jnp.float32), axis=-1)
    score_grad = (probs * (prob_grad - jnp.transpose(delta)[:, :, None])).astype(jnp.bfloat16)
    query_parts = (
        jnp.einsum("hbt,the->bhe", score_grad, key_rows, preferred_element_type=jnp.float32) * scale
    )
    key_grad = (
        jnp.einsum("hbt,bhe->the", score_grad, query_rows, preferred_element_type=jnp.float32)
        * scale
    )
    return (query_parts, key_grad, value_grad)


def on_device(
    layer_input,
    segment_ids,
    norm1_gain,
    norm1_shift,
    qkv_weight,
    qkv_bias,
    dense_weight,
    dense_bias,
    norm2_gain,
    norm2_shift,
    inner_weight,
    inner_bias,
    outer_weight,
    outer_bias,
    out_cotangent,
):
    gathered = (
        lax.all_gather(norm1_gain, "dp", axis=0, tiled=True),
        lax.all_gather(norm1_shift, "dp", axis=0, tiled=True),
        lax.all_gather(qkv_weight, "dp", axis=0, tiled=True),
        lax.all_gather(qkv_bias, "dp", axis=0, tiled=True),
        lax.all_gather(dense_weight, "dp", axis=0, tiled=True),
        lax.all_gather(dense_bias, "dp", axis=0, tiled=True),
        lax.all_gather(norm2_gain, "dp", axis=0, tiled=True),
        lax.all_gather(norm2_shift, "dp", axis=0, tiled=True),
        lax.all_gather(inner_weight, "dp", axis=0, tiled=True),
        lax.all_gather(inner_bias, "dp", axis=0, tiled=True),
        lax.all_gather(outer_weight, "dp", axis=0, tiled=True),
        lax.all_gather(outer_bias, "dp", axis=0, tiled=True),
    )
    (
        gain_one,
        shift_one,
        qkv_full,
        qkv_bias_full,
        dense_full,
        dense_bias_full,
        gain_two,
        shift_two,
        inner_full,
        inner_bias_full,
        outer_full,
        outer_bias_full,
    ) = gathered
    local_heads = qkv_full.shape[1] // (3 * HD)
    head_index = lax.axis_index("tensor") * local_heads + jnp.arange(local_heads, dtype=jnp.int32)
    head_slopes = jnp.exp2(-8.0 * (head_index.astype(jnp.float32) + 1.0) / H)
    segment_row = segment_ids[0]
    bias_pairs = qkv_bias_full.astype(jnp.float32).reshape(local_heads, 2, HD)
    bias_three = jnp.stack(
        [bias_pairs[:, 0], jnp.zeros_like(bias_pairs[:, 0]), bias_pairs[:, 1]], axis=1
    ).reshape(-1)
    normed_one, hat_one, inv_one = layer_norm(layer_input, gain_one, shift_one)
    norm_rows = lax.all_gather(normed_one.astype(jnp.bfloat16), "tensor", axis=0, tiled=True)
    group_rows = norm_rows.shape[0]
    projected = (
        jnp.dot(norm_rows, qkv_full, preferred_element_type=jnp.float32) + bias_three
    ).astype(jnp.bfloat16)
    projected = projected.reshape(group_rows, local_heads, 3, HD)
    query_rows = projected[:, :, 0]
    key_rows = projected[:, :, 1]
    value_rows = projected[:, :, 2]
    context, log_total = attend_forward(query_rows, key_rows, value_rows, segment_row, head_slopes)
    context_flat = context.reshape(group_rows, local_heads * HD)
    attn_part = lax.psum_scatter(
        cross_product(context_flat, dense_full).astype(jnp.bfloat16),
        "tensor",
        scatter_dimension=0,
        tiled=True,
    ).astype(jnp.float32)
    middle = layer_input + attn_part + dense_bias_full.astype(jnp.float32)
    normed_two, hat_two, inv_two = layer_norm(middle, gain_two, shift_two)
    mid_rows = lax.all_gather(normed_two.astype(jnp.bfloat16), "tensor", axis=0, tiled=True)
    pre_act = jnp.dot(
        mid_rows, inner_full, preferred_element_type=jnp.float32
    ) + inner_bias_full.astype(jnp.float32)
    act_value, act_slope = gelu_parts(pre_act)
    act_low = act_value.astype(jnp.bfloat16)
    layer_output = (
        middle
        + lax.psum_scatter(
            cross_product(act_low, outer_full).astype(jnp.bfloat16),
            "tensor",
            scatter_dimension=0,
            tiled=True,
        ).astype(jnp.float32)
        + outer_bias_full.astype(jnp.float32)
    )
    back_set = (
        lax.all_gather(norm1_gain, "dp", axis=0, tiled=True),
        lax.all_gather(qkv_weight, "dp", axis=0, tiled=True),
        lax.all_gather(dense_weight, "dp", axis=0, tiled=True),
        lax.all_gather(norm2_gain, "dp", axis=0, tiled=True),
        lax.all_gather(inner_weight, "dp", axis=0, tiled=True),
        lax.all_gather(outer_weight, "dp", axis=0, tiled=True),
    )
    gain_back_one, qkv_back, dense_back, gain_back_two, inner_back, outer_back = back_set
    cot_rows = lax.all_gather(out_cotangent.astype(jnp.bfloat16), "tensor", axis=0, tiled=True)
    outer_grad = rows_product(cot_rows, act_low)
    pre_grad = jnp.dot(cot_rows, outer_back, preferred_element_type=jnp.float32) * act_slope
    inner_bias_grad = jnp.sum(pre_grad, axis=0)
    pre_low = pre_grad.astype(jnp.bfloat16)
    inner_grad = rows_product(mid_rows, pre_low)
    mid_grad = lax.psum_scatter(
        cross_product(pre_low, inner_back).astype(jnp.bfloat16),
        "tensor",
        scatter_dimension=0,
        tiled=True,
    ).astype(jnp.float32)
    gain_two_grad = jnp.sum(mid_grad * hat_two, axis=0)
    shift_two_grad = jnp.sum(mid_grad, axis=0)
    middle_grad = out_cotangent + norm_back(mid_grad, hat_two, inv_two, gain_back_two)
    dense_bias_grad = jnp.sum(middle_grad, axis=0)
    outer_bias_grad = jnp.sum(out_cotangent, axis=0)
    middle_rows = lax.all_gather(middle_grad.astype(jnp.bfloat16), "tensor", axis=0, tiled=True)
    dense_grad = rows_product(middle_rows, context_flat)
    context_grad = jnp.dot(middle_rows, dense_back, preferred_element_type=jnp.float32).astype(
        jnp.bfloat16
    )
    context_grad = context_grad.reshape(group_rows, local_heads, HD)
    query_grad, key_grad, value_grad = attend_backward(
        query_rows, key_rows, value_rows, context, context_grad, log_total, segment_row, head_slopes
    )
    qkv_grad = jnp.stack([query_grad, key_grad, value_grad], axis=2).reshape(
        group_rows, local_heads * 3 * HD
    )
    bias_sums = jnp.sum(qkv_grad, axis=0).reshape(local_heads, 3, HD)
    qkv_bias_grad = jnp.stack([bias_sums[:, 0], bias_sums[:, 2]], axis=1).reshape(-1)
    qkv_low = qkv_grad.astype(jnp.bfloat16)
    qkv_weight_grad = rows_product(norm_rows, qkv_low)
    first_grad = lax.psum_scatter(
        cross_product(qkv_low, qkv_back).astype(jnp.bfloat16),
        "tensor",
        scatter_dimension=0,
        tiled=True,
    ).astype(jnp.float32)
    gain_one_grad = jnp.sum(first_grad * hat_one, axis=0)
    shift_one_grad = jnp.sum(first_grad, axis=0)
    input_grad = middle_grad + norm_back(first_grad, hat_one, inv_one, gain_back_one)
    small_sums = lax.psum(
        (
            gain_one_grad,
            shift_one_grad,
            dense_bias_grad,
            gain_two_grad,
            shift_two_grad,
            outer_bias_grad,
        ),
        "tensor",
    )
    everything = (
        lax.psum_scatter(
            small_sums[0].astype(jnp.bfloat16), "dp", scatter_dimension=0, tiled=True
        ).astype(jnp.float32),
        lax.psum_scatter(
            small_sums[1].astype(jnp.bfloat16), "dp", scatter_dimension=0, tiled=True
        ).astype(jnp.float32),
        lax.psum_scatter(
            qkv_weight_grad.astype(jnp.bfloat16), "dp", scatter_dimension=0, tiled=True
        ).astype(jnp.float32),
        lax.psum_scatter(
            qkv_bias_grad.astype(jnp.bfloat16), "dp", scatter_dimension=0, tiled=True
        ).astype(jnp.float32),
        lax.psum_scatter(
            dense_grad.astype(jnp.bfloat16), "dp", scatter_dimension=0, tiled=True
        ).astype(jnp.float32),
        lax.psum_scatter(
            small_sums[2].astype(jnp.bfloat16), "dp", scatter_dimension=0, tiled=True
        ).astype(jnp.float32),
        lax.psum_scatter(
            small_sums[3].astype(jnp.bfloat16), "dp", scatter_dimension=0, tiled=True
        ).astype(jnp.float32),
        lax.psum_scatter(
            small_sums[4].astype(jnp.bfloat16), "dp", scatter_dimension=0, tiled=True
        ).astype(jnp.float32),
        lax.psum_scatter(
            inner_grad.astype(jnp.bfloat16), "dp", scatter_dimension=0, tiled=True
        ).astype(jnp.float32),
        lax.psum_scatter(
            inner_bias_grad.astype(jnp.bfloat16), "dp", scatter_dimension=0, tiled=True
        ).astype(jnp.float32),
        lax.psum_scatter(
            outer_grad.astype(jnp.bfloat16), "dp", scatter_dimension=0, tiled=True
        ).astype(jnp.float32),
        lax.psum_scatter(
            small_sums[5].astype(jnp.bfloat16), "dp", scatter_dimension=0, tiled=True
        ).astype(jnp.float32),
    )
    return (
        layer_output,
        input_grad,
        everything[0],
        everything[1],
        everything[2],
        everything[3],
        everything[4],
        everything[5],
        everything[6],
        everything[7],
        everything[8],
        everything[9],
        everything[10],
        everything[11],
    )


def solution(mesh):
    in_specs = (
        P(("dp", "tensor"), None),
        P("dp", None),
        P("dp"),
        P("dp"),
        P("dp", "tensor"),
        P(("tensor", "dp")),
        P("dp", "tensor"),
        P("dp"),
        P("dp"),
        P("dp"),
        P("dp", "tensor"),
        P(("tensor", "dp")),
        P("dp", "tensor"),
        P("dp"),
        P(("dp", "tensor"), None),
    )
    out_specs = (
        P(("dp", "tensor"), None),
        P(("dp", "tensor"), None),
        P("dp"),
        P("dp"),
        P("dp", "tensor"),
        P(("tensor", "dp")),
        P("dp", "tensor"),
        P("dp"),
        P("dp"),
        P("dp"),
        P("dp", "tensor"),
        P(("tensor", "dp")),
        P("dp", "tensor"),
        P("dp"),
    )
    return jax.shard_map(
        on_device, mesh=mesh, in_specs=in_specs, out_specs=out_specs, check_vma=False
    )
```

profile of v0, /device:TPU:0, one launch (start us, length us, event | category | flops | bytes accessed | tf_op | source)
XLA Modules:
  0.0 754.2 jit_solution(11036563063567816782)
XLA Ops:
  14.3 63.0 %all-reduce.17 = (bf16[1024]{0:T(1024)(128)(2,1)S(1)}, bf16[1024]{0:T(1024)(128)(2,1)S(1)}, bf16[1024]{0:T(1024)(128)(2,1)S(1)}, bf16[1024]{0:T(1024)(128)(2,1)S...) all-reduce(bf16[1024]{0:T(1024)(128)(2,1)S(1)} %dynamic-update-slic, ...), channel_id=1, replica_groups=mesh['dp'=16,'tensor'=2] {'dp'}, use_global_device_ids=true, to_apply=%add.1 | all-reduce | flops 6144 | bytes 24576
  78.6 1.5 multiply_reduce_fusion.2
  80.1 2.3 add_convert_fusion.1
  84.6 16.5 %all-gather.10.cloned.1.call-done = bf16[512,1024]{1,0:T(8,128)(2,1)} async-done(((bf16[256,1024]{1,0:T(8,128)(2,1)}), bf16[512,1024]{1,0:T(8,128)(2,1)}) %all-gather.10.cloned.1.call-update) | async-done | bytes 1048592 | tf_op jit(solution)/shard_map/all_gather | solution.py:155
  101.1 47.8 %all-gather.12.cloned.1.call-done = bf16[1024,1536]{1,0:T(8,128)(2,1)} async-done(((bf16[64,1536]{1,0:T(8,128)(2,1)}), bf16[1024,1536]{1,0:T(8,128)(2,1)}) %all-gather.12.cloned.1.call-update) | async-done | bytes 3145744 | tf_op jit(solution)/shard_map/all_gather | solution.py:121
  148.9 5.2 fusion.9
  154.0 1.7 copy.60
  155.8 2.4 fusion.42
  159.4 2.0 copy-done
  161.4 1.4 convolution_convert_fusion.7
  162.9 24.4 %all-gather.14.cloned.1.call-done = bf16[1024,512]{1,0:T(8,128)(2,1)} async-done(((bf16[64,512]{1,0:T(8,128)(2,1)}), bf16[1024,512]{1,0:T(8,128)(2,1)}) %all-gather.14.cloned.1.call-update) | async-done | bytes 1048592 | tf_op jit(solution)/shard_map/all_gather | solution.py:123
  187.3 3.0 convolution_convert_fusion.4
  191.0 18.8 %reduce-scatter.11.cloned.1.call-done = bf16[256,1024]{1,0:T(8,128)(2,1)} async-done(((bf16[512,1024]{1,0:T(8,128)(2,1)}), bf16[256,1024]{1,0:T(8,128)(2,1)}) %reduce-scatter.11.cloned.1.call-update) | async-done | bytes 524304 | tf_op jit(solution)/shard_map/reduce_scatter | solution.py:166
  214.2 22.0 %all-gather = bf16[16,1,128]{2,1,0:T(2,128)(2,1)S(1)} all-gather(bf16[1,1,128]{2,1,0:T(2,128)(2,1)S(1)} %bitcast.96), channel_id=1, replica_groups=mesh['dp'=16,'tensor'=2] {'dp'}, dimensions={0}, use_global_device_ids=true | all-gather | bytes 4352 | tf_op jit(solution)/shard_map/all_gather | solution.py:128
  236.2 26.1 %all-gather.18.cloned.1.call-done = bf16[1024,2048]{1,0:T(8,128)(2,1)} async-done(((bf16[64,2048]{1,0:T(8,128)(2,1)}), bf16[1024,2048]{1,0:T(8,128)(2,1)}) %all-gather.18.cloned.1.call-update) | async-done | bytes 4194320 | tf_op jit(solution)/shard_map/all_gather | solution.py:127
  262.3 21.8 %all-gather.16.cloned.1.call-done = bf16[512,1024]{1,0:T(8,128)(2,1)} async-done(((bf16[256,1024]{1,0:T(8,128)(2,1)}), bf16[512,1024]{1,0:T(8,128)(2,1)}) %all-gather.16.cloned.1.call-update) | async-done | bytes 1048592 | tf_op jit(solution)/shard_map/all_gather | solution.py:174
  284.1 6.8 fusion.44
  290.9 16.6 %all-gather.22.cloned.1.call-done = bf16[512,1024]{1,0:T(8,128)(2,1)} async-done(((bf16[256,1024]{1,0:T(8,128)(2,1)}), bf16[512,1024]{1,0:T(8,128)(2,1)}) %all-gather.22.cloned.1.call-update) | async-done | bytes 1048592 | tf_op jit(solution)/shard_map/all_gather | solution.py:199
  307.5 52.6 %all-gather.20.cloned.1.call-done = bf16[1024,2048]{1,0:T(8,128)(2,1)} async-done(((bf16[64,2048]{1,0:T(8,128)(2,1)}), bf16[1024,2048]{1,0:T(8,128)(2,1)}) %all-gather.20.cloned.1.call-update) | async-done | bytes 4194320 | tf_op jit(solution)/shard_map/all_gather | solution.py:129
  360.1 8.4 %fusion.43 = (bf16[2048]{0:T(1024)(128)(2,1)S(1)}, bf16[512,2048]{1,0:T(8,128)(2,1)S(1)}) fusion(f32[512,2048]{1,0:T(8,128)} %fusion.44, f32[2048]{0:T(1024)S(1)} %bitcast.93, bf16[512,1024]{1,0:T(8,128)(2,1)} %all-gather.22.cloned.1.call-done, bf16[1024,2048]{1,0:T(8,128)(2,1)} %all-gather.20.cloned.1.call-done), kind=kOutput, calls=%fused_computation.102 | convolution fusion | flops 2169501696 | bytes 11546624 | tf_op jit(solution)/shard_map/dot_general | solution.py:201
  369.9 3.3 convolution_convert_fusion.5
  373.3 19.0 %reduce-scatter.15.cloned.1.call-done = bf16[256,1024]{1,0:T(8,128)(2,1)} async-done(((bf16[512,1024]{1,0:T(8,128)(2,1)}), bf16[256,1024]{1,0:T(8,128)(2,1)}) %reduce-scatter.15.cloned.1.call-update) | async-done | bytes 524304 | tf_op jit(solution)/shard_map/reduce_scatter | solution.py:205
  392.3 1.6 fusion.30
  393.9 1.8 fusion.35
  396.6 21.4 %all-gather.24.cloned.1.call-done = bf16[512,1024]{1,0:T(8,128)(2,1)} async-done(((bf16[256,1024]{1,0:T(8,128)(2,1)}), bf16[512,1024]{1,0:T(8,128)(2,1)}) %all-gather.24.cloned.1.call-update) | async-done | bytes 1048592 | tf_op jit(solution)/shard_map/all_gather | solution.py:216
  418.0 3.1 convolution_convert_fusion.3
  421.3 2.6 multiply_reduce_fusion
  424.0 4.9 multiply_convert_fusion
  436.0 2.8 convolution_convert_fusion.2
  438.9 7.3 convolution_convert_fusion.6
  446.4 7.9 %convert_bitcast_fusion = bf16[1024,2048]{0,1:T(8,128)(2,1)} fusion(bf16[512,1024]{1,0:T(8,128)(2,1)} %all-gather.22.cloned.1.call-done, f32[512,2048]{1,0:T(8,128)} %fusion.44, f32[2048]{0:T(1024)S(1)} %bitcast.95), kind=kOutput, calls=%fused_computation.15 | convolution fusion | flops 2160066560 | bytes 9445376 | tf_op jit(solution)/shard_map/dot_general | solution.py:40
  454.3 6.5 copy.77
  460.9 6.3 convolution_convert_fusion
  467.3 5.3 convolution_convert_fusion.1
  474.2 2.2 fusion.10
  476.5 2.9 reduce-scatter.21.cloned.1.call-done
  479.4 1.5 convert_element_type.230
  480.9 20.5 %reduce-scatter.17.cloned.1.call-done = bf16[256,1024]{1,0:T(8,128)(2,1)} async-done(((bf16[512,1024]{1,0:T(8,128)(2,1)}), bf16[256,1024]{1,0:T(8,128)(2,1)}) %reduce-scatter.17.cloned.1.call-update) | async-done | bytes 524304 | tf_op jit(solution)/shard_map/reduce_scatter | solution.py:232
  501.4 1.6 fusion.31
  503.0 7.1 all-reduce.15
  510.1 60.0 %all-reduce.16 = (bf16[1024]{0:T(1024)(128)(2,1)S(1)}, bf16[1024]{0:T(1024)(128)(2,1)S(1)}, bf16[1024]{0:T(1024)(128)(2,1)S(1)}, bf16[1024]{0:T(1024)(128)(2,1)S...) all-reduce(bf16[1024]{0:T(1024)(128)(2,1)S(1)} %dynamic-update-slic, ...), channel_id=1, replica_groups=mesh['dp'=16,'tensor'=2] {'dp'}, use_global_device_ids=true, to_apply=%add.6 | all-reduce | flops 10240 | bytes 40960
  574.8 2.2 add_add_fusion
  577.0 2.4 fusion.24
  579.4 21.6 %reduce-scatter.25.cloned.1.call-done = bf16[64,2048]{1,0:T(8,128)(2,1)} async-done(((bf16[1024,2048]{1,0:T(8,128)(2,1)}), bf16[64,2048]{1,0:T(8,128)(2,1)}) %reduce-scatter.25.cloned.1.call-update) | async-done | bytes 262160
  603.2 73.4 %reduce-scatter.23.cloned.1.call-done = bf16[64,2048]{1,0:T(8,128)(2,1)} async-done(((bf16[1024,2048]{1,0:T(8,128)(2,1)}), bf16[64,2048]{1,0:T(8,128)(2,1)}) %reduce-scatter.23.cloned.1.call-update) | async-done | bytes 262160 | tf_op jit(solution)/shard_map/reduce_scatter | solution.py:277
  676.6 1.8 convert_element_type.238
  678.4 67.3 %reduce-scatter.19.cloned.1.call-done = bf16[64,1536]{1,0:T(8,128)(2,1)} async-done(((bf16[1024,1536]{1,0:T(8,128)(2,1)}), bf16[64,1536]{1,0:T(8,128)(2,1)}) %reduce-scatter.19.cloned.1.call-update) | async-done | bytes 196624 | tf_op jit(solution)/shard_map/reduce_scatter | solution.py:259
  745.7 1.7 convert_element_type.226
  (133 shorter events, 33.5 us)
Async XLA Ops:
  7.2 77.2 %copy-start.10 = (s32[1,512]{1,0:T(1,128)S(1)}, s32[1,512]{1,0:T(1,128)}, u32[]{:S(2)}) copy-start(s32[1,512]{1,0:T(1,128)} %param.16) | copy-start | bytes 6148
  7.2 93.9 %all-gather.10.cloned.1.call-start = ((), (), s32[]{:S(2)}) async-start(), calls=%async_computation.8 | async-start | bytes 1572864 | tf_op jit(solution)/shard_map/all_gather | solution.py:155
  82.4 66.4 %all-gather.12.cloned.1.call-start = ((), (), s32[]{:S(2)}) async-start(), calls=%async_computation.9 | async-start | bytes 3342336 | tf_op jit(solution)/shard_map/all_gather | solution.py:121
  83.2 104.2 %all-gather.14.cloned.1.call-start = ((), (), s32[]{:S(2)}) async-start(), calls=%async_computation.10 | async-start | bytes 1114112 | tf_op jit(solution)/shard_map/all_gather | solution.py:123
  83.9 125.9 %reduce-scatter.11.cloned.1.call-start = ((), (), s32[]{:S(2)}) async-start(), calls=%async_computation.11 | async-start | bytes 1572864 | tf_op jit(solution)/shard_map/reduce_scatter | solution.py:166
  155.7 3.7 copy-start.5
  158.2 3.2 copy-start
  162.8 28.1 %copy-start.9 = (bf16[8,64,512]{2,1,0:T(8,128)(2,1)}, bf16[8,64,512]{2,1,0:T(8,128)(2,1)S(1)}, u32[]{:S(2)}) copy-start(bf16[8,64,512]{2,1,0:T(8,128)(2,1)S(1)} %convolution_convert_fusion.7) | copy-start | bytes 1572868
  162.9 46.9 %copy-start.1 = (f32[256,1024]{1,0:T(8,128)S(1)}, f32[256,1024]{1,0:T(8,128)}, u32[]{:S(2)}) copy-start(f32[256,1024]{1,0:T(8,128)} %param.15) | copy-start | bytes 3145732
  190.3 22.2 %copy-start.7 = (f32[256,1024]{1,0:T(8,128)S(1)}, f32[256,1024]{1,0:T(8,128)}, u32[]{:S(2)}) copy-start(f32[256,1024]{1,0:T(8,128)} %param.29) | copy-start | bytes 3145732
  190.3 23.9 %copy-start.11 = (bf16[128]{0:T(256)(128)(2,1)S(1)}, bf16[128]{0:T(256)(128)(2,1)}, u32[]{:S(2)}) copy-start(bf16[128]{0:T(256)(128)(2,1)} %param.26) | copy-start | bytes 772
  190.3 72.0 %all-gather.18.cloned.1.call-start = ((), (), s32[]{:S(2)}) async-start(), calls=%async_computation.13 | async-start | bytes 4456448 | tf_op jit(solution)/shard_map/all_gather | solution.py:127
  190.9 93.2 %all-gather.16.cloned.1.call-start = ((), (), s32[]{:S(2)}) async-start(), calls=%async_computation.12 | async-start | bytes 1572864 | tf_op jit(solution)/shard_map/all_gather | solution.py:174
  212.4 95.1 %all-gather.22.cloned.1.call-start = ((), (), s32[]{:S(2)}) async-start(), calls=%async_computation.16 | async-start | bytes 1572864 | tf_op jit(solution)/shard_map/all_gather | solution.py:199
  213.4 146.7 %all-gather.20.cloned.1.call-start = ((), (), s32[]{:S(2)}) async-start(), calls=%async_computation.14 | async-start | bytes 4456448 | tf_op jit(solution)/shard_map/all_gather | solution.py:129
  214.1 178.2 %reduce-scatter.15.cloned.1.call-start = ((), (), s32[]{:S(2)}) async-start(), calls=%async_computation.17 | async-start | bytes 1572864 | tf_op jit(solution)/shard_map/reduce_scatter | solution.py:205
  360.1 9.8 %copy-start.12 = (bf16[1024,2048]{1,0:T(8,128)(2,1)S(1)}, bf16[1024,2048]{1,0:T(8,128)(2,1)}, u32[]{:S(2)}) copy-start(bf16[1024,2048]{1,0:T(8,128)(2,1)} %all-gather.18.cloned.1.call-done) | copy-start | bytes 12582916
  368.5 1.4 copy-start.15
  373.3 44.8 %all-gather.24.cloned.1.call-start = ((), (), s32[]{:S(2)}) async-start(), calls=%async_computation.18 | async-start | bytes 1572864 | tf_op jit(solution)/shard_map/all_gather | solution.py:216
  396.6 82.8 %reduce-scatter.21.cloned.1.call-start = ((), (), s32[]{:S(2)}) async-start(), calls=%async_computation.21 | async-start | bytes 1114112 | tf_op jit(solution)/shard_map/reduce_scatter | solution.py:265
  421.1 80.3 %reduce-scatter.17.cloned.1.call-start = ((), (), s32[]{:S(2)}) async-start(), calls=%async_computation.19 | async-start | bytes 1572864 | tf_op jit(solution)/shard_map/reduce_scatter | solution.py:232
  421.3 9.7 %slice-start = ((s8[8388608]{0:T(1024)(128)(4,1)}), s8[4194304]{0:T(1024)(128)(4,1)S(1)}, s32[]{:S(2)}) async-start(s8[8388608]{0:T(1024)(128)(4,1)} %bitcast.78), calls=%async_computation.24 | async-start | bytes 8388608
  424.0 4.9 copy-start.6
  424.0 7.1 slice-start.1
  430.3 2.2 copy-start.3
  431.1 1.4 copy-start.4
  432.5 1.0 copy-start.2
  433.5 2.5 copy-start.13
  434.0 1.2 copy-start.8
  438.9 135.9 %reduce-scatter.13.cloned.1.call-start = ((), (), s32[]{:S(2)}) async-start(), calls=%async_computation.15 | async-start | bytes 1572864 | tf_op jit(solution)/shard_map/reduce_scatter | solution.py:182
  446.2 154.8 %reduce-scatter.25.cloned.1.call-start = ((), (), s32[]{:S(2)}) async-start(), calls=%async_computation.23 | async-start | bytes 4456448
  460.8 215.8 %reduce-scatter.23.cloned.1.call-start = ((), (), s32[]{:S(2)}) async-start(), calls=%async_computation.22 | async-start | bytes 4456448 | tf_op jit(solution)/shard_map/reduce_scatter | solution.py:277
  467.2 6.7 copy-start.14
  467.2 278.5 %reduce-scatter.19.cloned.1.call-start = ((), (), s32[]{:S(2)}) async-start(), calls=%async_computation.20 | async-start | bytes 3342336 | tf_op jit(solution)/shard_map/reduce_scatter | solution.py:259
Sparse Core Ops, SparseCore 0:
  82.5 18.5 all-gather.9
  103.4 45.4 all-gather.11
  151.0 36.2 all-gather.13
  190.4 19.3 reduce-scatter.10
  211.8 50.4 all-gather.17
  264.3 19.7 all-gather.15
  286.2 21.2 all-gather.21
  309.7 50.3 all-gather.19
  373.4 18.9 reduce-scatter.14
  396.7 21.2 all-gather.23
  421.6 57.6 reduce-scatter.20
  482.0 19.3 reduce-scatter.16
  504.2 20.3 reduce-scatter.12
  528.4 72.6 reduce-scatter.24
  604.7 71.8 reduce-scatter.22
  680.3 65.3 reduce-scatter.18
where the time goes:
time: 763 us; the launch traced here: 754 us
  waiting for transfers between devices  454 us (60%)
  blocking collectives  152 us (20%)
  matrix products  74.2 us (10%)
  other arithmetic  32.8 us (4%)
  local copies, waits for them, and re-layouts  23.9 us (3%)
  between operations  16.6 us (2%)
    unnamed x2, blocking collectives  123 us
    reduce_scatter x1, waiting for transfers between devices, on_device(): lax.psum_scatter(inner_grad.astype(jnp.bfloat16), 'dp', scatter_dimension...  73.4 us
    reduce_scatter x1, waiting for transfers between devices, on_device(): lax.psum_scatter(qkv_weight_grad.astype(jnp.bfloat16), 'dp', scatter_dime...  67.3 us
    all_gather x1, waiting for transfers between devices, on_device(): lax.all_gather(outer_weight, 'dp', axis=0, tiled=True)  52.6 us
    all_gather x1, waiting for transfers between devices, on_device(): lax.all_gather(qkv_weight, 'dp', axis=0, tiled=True)  47.8 us
    all_gather x1, waiting for transfers between devices, on_device(): lax.all_gather(inner_weight, 'dp', axis=0, tiled=True)  26.1 us
    unnamed x17, waiting for transfers between devices  24.5 us
    all_gather x1, waiting for transfers between devices, on_device(): lax.all_gather(dense_weight, 'dp', axis=0, tiled=True)  24.4 us
  transfers between devices with their start and end apart: 16, of which 15 were waited for; matrix products, arithmetic and copies ran while one was open for 12% of the time, Pallas kernels for 0%

commit v1 on v0

--- a/solution.py
+++ b/solution.py
@@ -8,6 +8,18 @@
 EPSILON = 1e-05
 GELU_C = 0.7978845608028654
 GELU_K = 0.044715
+
+
+def collect(x, axis, dim):
+    ways, here, step = (lax.axis_size(axis), lax.axis_index(axis), x.shape[dim])
+    line, have = (x, 1)
+    while have < ways:
+        line = jnp.concatenate(
+            [line, lax.ppermute(line, axis, [(d, (d - have) % ways) for d in range(ways)])],
+            axis=dim,
+        )
+        have = 2 * have
+    return jnp.roll(line, here * step, axis=dim)
 
 
 def layer_norm(row_data, gain, shift):
@@ -126,7 +138,7 @@
         lax.all_gather(norm2_shift, "dp", axis=0, tiled=True),
         lax.all_gather(inner_weight, "dp", axis=0, tiled=True),
         lax.all_gather(inner_bias, "dp", axis=0, tiled=True),
-        lax.all_gather(outer_weight, "dp", axis=0, tiled=True),
+        collect(outer_weight, "dp", 0),
         lax.all_gather(outer_bias, "dp", axis=0, tiled=True),
     )
     (

time: 763 us -> 826 us (1.083)
  waiting for transfers between devices: 454 us -> 486 us
  local copies, waits for them, and re-layouts: 23.9 us -> 42.4 us
    ppermute x0 -> x4, waiting for transfers between devices: none -> 105 us  [collect(): lax.ppermute(line, axis, [(d, (d - have) % ways) for d in range(ways)])]
    all_gather x1, waiting for transfers between devices: 21.4 us -> 0.01 us  [on_device(): lax.all_gather(middle_grad.astype(jnp.bfloat16), 'tensor', axis=0, tiled=...]
    reduce_scatter x1, waiting for transfers between devices: 20.5 us -> 0.01 us  [on_device(): lax.psum_scatter(cross_product(qkv_low, qkv_back).astype(jnp.bfloat16), '...]
    reduce_scatter x1, waiting for transfers between devices: 19 us -> 0.01 us  [on_device(): lax.psum_scatter(cross_product(pre_low, inner_back).astype(jnp.bfloat16),...]
    unnamed x54 -> x75, local copies, waits for them, and re-layouts: 21.7 us -> 37 us
  transfers between devices with their start and end apart: 16 -> 20, of which waited for: 15 -> 15; matrix products, arithmetic and copies ran while one was open for 12% -> 14% of each run, Pallas kernels for 0% -> 0%
where the time goes in v1:
time: 826 us; the launch traced here: 817 us
  waiting for transfers between devices  486 us (59%)
  blocking collectives  156 us (19%)
  matrix products  72.7 us (9%)
  local copies, waits for them, and re-layouts  42.4 us (5%)
  other arithmetic  36.9 us (4%)
  between operations  16.6 us (2%)
    unnamed x2, blocking collectives  124 us
    ppermute x4, waiting for transfers between devices, collect(): lax.ppermute(line, axis, [(d, (d - have) % ways) for d in range(ways)])  105 us
    reduce_scatter x1, waiting for transfers between devices, on_device(): lax.psum_scatter(inner_grad.astype(jnp.bfloat16), 'dp', scatter_dimension...  73.4 us
    reduce_scatter x1, waiting for transfers between devices, on_device(): lax.psum_scatter(qkv_weight_grad.astype(jnp.bfloat16), 'dp', scatter_dime...  67.3 us
    all_gather x1, waiting for transfers between devices, on_device(): lax.all_gather(outer_weight, 'dp', axis=0, tiled=True)  52.6 us
    all_gather x1, waiting for transfers between devices, on_device(): lax.all_gather(qkv_weight, 'dp', axis=0, tiled=True)  47.8 us
    unnamed x75, local copies, waits for them, and re-layouts  37 us
    all_gather x1, waiting for transfers between devices, on_device(): lax.all_gather(inner_weight, 'dp', axis=0, tiled=True)  26.1 us
  transfers between devices with their start and end apart: 20, of which 15 were waited for; matrix products, arithmetic and copies ran while one was open for 14% of the time, Pallas kernels for 0%

profile of v1, /device:TPU:0, one launch (start us, length us, event | category | flops | bytes accessed | tf_op | source)
XLA Modules:
  0.0 817.2 jit_solution(8607421593582167436)
XLA Ops:
  14.3 63.0 %all-reduce.17 = (bf16[1024]{0:T(1024)(128)(2,1)S(1)}, bf16[1024]{0:T(1024)(128)(2,1)S(1)}, bf16[1024]{0:T(1024)(128)(2,1)S(1)}, bf16[1024]{0:T(1024)(128)(2,1)S...) all-reduce(bf16[1024]{0:T(1024)(128)(2,1)S(1)} %dynamic-update-slic, ...), channel_id=1, replica_groups=mesh['dp'=16,'tensor'=2] {'dp'}, use_global_device_ids=true, to_apply=%add.1 | all-reduce | flops 6144 | bytes 24576
  80.1 2.3 add_convert_fusion.1
  84.6 16.5 %all-gather.10.cloned.1.call-done = bf16[512,1024]{1,0:T(8,128)(2,1)} async-done(((bf16[256,1024]{1,0:T(8,128)(2,1)}), bf16[512,1024]{1,0:T(8,128)(2,1)}) %all-gather.10.cloned.1.call-update) | async-done | bytes 1048592 | tf_op jit(solution)/shard_map/all_gather | solution.py:167
  101.1 47.8 %all-gather.12.cloned.1.call-done = bf16[1024,1536]{1,0:T(8,128)(2,1)} async-done(((bf16[64,1536]{1,0:T(8,128)(2,1)}), bf16[1024,1536]{1,0:T(8,128)(2,1)}) %all-gather.12.cloned.1.call-update) | async-done | bytes 3145744 | tf_op jit(solution)/shard_map/all_gather | solution.py:133
  148.9 5.2 fusion.11
  155.8 2.4 fusion.48
  159.4 2.1 copy-done
  163.0 24.4 %all-gather.14.cloned.1.call-done = bf16[1024,512]{1,0:T(8,128)(2,1)} async-done(((bf16[64,512]{1,0:T(8,128)(2,1)}), bf16[1024,512]{1,0:T(8,128)(2,1)}) %all-gather.14.cloned.1.call-update) | async-done | bytes 1048592 | tf_op jit(solution)/shard_map/all_gather | solution.py:135
  187.3 3.0 convolution_convert_fusion.4
  191.0 18.8 %reduce-scatter.11.cloned.1.call-done = bf16[256,1024]{1,0:T(8,128)(2,1)} async-done(((bf16[512,1024]{1,0:T(8,128)(2,1)}), bf16[256,1024]{1,0:T(8,128)(2,1)}) %reduce-scatter.11.cloned.1.call-update) | async-done | bytes 524304 | tf_op jit(solution)/shard_map/reduce_scatter | solution.py:178
  214.2 21.9 %all-gather = bf16[16,1,128]{2,1,0:T(2,128)(2,1)S(1)} all-gather(bf16[1,1,128]{2,1,0:T(2,128)(2,1)S(1)} %bitcast.95), channel_id=1, replica_groups=mesh['dp'=16,'tensor'=2] {'dp'}, dimensions={0}, use_global_device_ids=true | all-gather | bytes 4352 | tf_op jit(solution)/shard_map/all_gather | solution.py:140
  236.2 26.1 %all-gather.18.cloned.1.call-done = bf16[1024,2048]{1,0:T(8,128)(2,1)} async-done(((bf16[64,2048]{1,0:T(8,128)(2,1)}), bf16[1024,2048]{1,0:T(8,128)(2,1)}) %all-gather.18.cloned.1.call-update) | async-done | bytes 4194320 | tf_op jit(solution)/shard_map/all_gather | solution.py:139
  262.3 21.8 %all-gather.16.cloned.1.call-done = bf16[512,1024]{1,0:T(8,128)(2,1)} async-done(((bf16[256,1024]{1,0:T(8,128)(2,1)}), bf16[512,1024]{1,0:T(8,128)(2,1)}) %all-gather.16.cloned.1.call-update) | async-done | bytes 1048592 | tf_op jit(solution)/shard_map/all_gather | solution.py:186
  284.1 6.9 fusion.50
  291.0 16.6 %all-gather.20.cloned.1.call-done = bf16[512,1024]{1,0:T(8,128)(2,1)} async-done(((bf16[256,1024]{1,0:T(8,128)(2,1)}), bf16[512,1024]{1,0:T(8,128)(2,1)}) %all-gather.20.cloned.1.call-update) | async-done | bytes 1048592 | tf_op jit(solution)/shard_map/all_gather | solution.py:211
  307.5 52.6 %all-gather.22.cloned.1.call-done = bf16[1024,2048]{1,0:T(8,128)(2,1)} async-done(((bf16[64,2048]{1,0:T(8,128)(2,1)}), bf16[1024,2048]{1,0:T(8,128)(2,1)}) %all-gather.22.cloned.1.call-update) | async-done | bytes 4194320 | tf_op jit(solution)/shard_map/all_gather | solution.py:208
  360.1 8.4 %fusion.49 = (bf16[2048]{0:T(1024)(128)(2,1)S(1)}, bf16[512,2048]{1,0:T(8,128)(2,1)S(1)}) fusion(f32[512,2048]{1,0:T(8,128)} %fusion.50, f32[2048]{0:T(1024)S(1)} %bitcast.92, bf16[512,1024]{1,0:T(8,128)(2,1)} %all-gather.20.cloned.1.call-done, bf16[1024,2048]{1,0:T(8,128)(2,1)} %all-gather.22.cloned.1.call-done), kind=kOutput, calls=%fused_computation.118 | convolution fusion | flops 2169501696 | bytes 11546624 | tf_op jit(solution)/shard_map/dot_general | solution.py:213
  369.8 3.3 convolution_convert_fusion.5
  375.0 3.9 collective-permute-done
  380.5 12.8 %collective-permute-done.1 = bf16[128,2048]{1,0:T(8,128)(2,1)S(1)} collective-permute-done((bf16[128,2048]{1,0:T(8,128)(2,1)S(1)}, bf16[128,2048]{1,0:T(8,128)(2,1)S(1)}, u32[]{:S(2)}, u32[]{:S(2)}) %collective-permute-start.1) | collective-permute-done | bytes 524320 | tf_op jit(solution)/shard_map/ppermute | solution.py:18
  397.3 1.8 fusion.41
  402.4 1.9 constant_dynamic-update-slice_fusion.7
  404.3 15.9 %collective-permute-done.2 = bf16[256,2048]{1,0:T(8,128)(2,1)} collective-permute-done((bf16[256,2048]{1,0:T(8,128)(2,1)}, bf16[256,2048]{1,0:T(8,128)(2,1)}, u32[]{:S(2)}, u32[]{:S(2)}) %collective-permute-start.2) | collective-permute-done | bytes 1048608 | tf_op jit(solution)/shard_map/ppermute | solution.py:18
  420.2 3.0 pad_maximum_fusion.1
  423.2 1.9 collective-permute-start.3
  425.1 2.4 constant_dynamic-update-slice_fusion.6
  427.5 3.1 convolution_convert_fusion.3
  430.8 2.6 multiply_reduce_fusion
  433.5 4.9 multiply_convert_fusion
  445.5 2.8 convolution_convert_fusion.2
  448.4 72.2 %collective-permute-done.3 = bf16[512,2048]{1,0:T(8,128)(2,1)} collective-permute-done((bf16[512,2048]{1,0:T(8,128)(2,1)}, bf16[512,2048]{1,0:T(8,128)(2,1)}, u32[]{:S(2)}, u32[]{:S(2)}) %collective-permute-start.3) | collective-permute-done | bytes 2097184 | tf_op jit(solution)/shard_map/ppermute | solution.py:18
  520.6 3.1 constant_dynamic-update-slice_fusion.5
  526.1 2.3 constant_dynamic-update-slice_fusion.1
  528.4 3.2 constant_dynamic-update-slice_fusion
  531.6 6.0 fusion.14
  537.9 7.7 convert_bitcast_fusion
  545.6 6.5 copy.77
  552.2 6.2 convolution_convert_fusion
  558.5 5.2 convolution_convert_fusion.1
  565.3 2.1 fusion.12
  570.7 9.5 %all-reduce.15 = (bf16[1024]{0:T(1024)(128)(2,1)S(1)}, bf16[1024]{0:T(1024)(128)(2,1)S(1)}, bf16[1024]{0:T(1024)(128)(2,1)S(1)}, bf16[1024]{0:T(1024)(128)(2,1)S...) all-reduce(f32[1024]{0:T(1024)S(1)} %get-tuple-element.72, ...), channel_id=1, replica_groups=mesh['dp'=16,'tensor'=2] {'tensor'}, use_global_device_ids=true, to_apply=%region_16.17 | all-reduce | flops 6144 | bytes 36864 | tf_op jit(solution)/shard_map/psum | solution.py:253
  580.2 61.2 %all-reduce.16 = (bf16[1024]{0:T(1024)(128)(2,1)S(1)}, bf16[1024]{0:T(1024)(128)(2,1)S(1)}, bf16[1024]{0:T(1024)(128)(2,1)S(1)}, bf16[1024]{0:T(1024)(128)(2,1)S...) all-reduce(bf16[1024]{0:T(1024)(128)(2,1)S(1)} %dynamic-update-slic, ...), channel_id=1, replica_groups=mesh['dp'=16,'tensor'=2] {'dp'}, use_global_device_ids=true, to_apply=%add.6 | all-reduce | flops 10240 | bytes 40960
  646.0 2.2 add_add_fusion
  648.2 2.4 fusion.29
  650.6 13.4 %reduce-scatter.25.cloned.1.call-done = bf16[64,2048]{1,0:T(8,128)(2,1)} async-done(((bf16[1024,2048]{1,0:T(8,128)(2,1)}), bf16[64,2048]{1,0:T(8,128)(2,1)}) %reduce-scatter.25.cloned.1.call-update) | async-done | bytes 262160
  666.3 73.4 %reduce-scatter.23.cloned.1.call-done = bf16[64,2048]{1,0:T(8,128)(2,1)} async-done(((bf16[1024,2048]{1,0:T(8,128)(2,1)}), bf16[64,2048]{1,0:T(8,128)(2,1)}) %reduce-scatter.23.cloned.1.call-update) | async-done | bytes 262160 | tf_op jit(solution)/shard_map/reduce_scatter | solution.py:289
  739.6 1.8 convert_element_type.238
  741.4 67.3 %reduce-scatter.19.cloned.1.call-done = bf16[64,1536]{1,0:T(8,128)(2,1)} async-done(((bf16[1024,1536]{1,0:T(8,128)(2,1)}), bf16[64,1536]{1,0:T(8,128)(2,1)}) %reduce-scatter.19.cloned.1.call-update) | async-done | bytes 196624 | tf_op jit(solution)/shard_map/reduce_scatter | solution.py:271
  (166 shorter events, 54.8 us)
Async XLA Ops:
  7.2 77.2 %copy-start.15 = (s32[1,512]{1,0:T(1,128)S(1)}, s32[1,512]{1,0:T(1,128)}, u32[]{:S(2)}) copy-start(s32[1,512]{1,0:T(1,128)} %param.16) | copy-start | bytes 6148
  7.2 93.9 %all-gather.10.cloned.1.call-start = ((), (), s32[]{:S(2)}) async-start(), calls=%async_computation.8 | async-start | bytes 1572864 | tf_op jit(solution)/shard_map/all_gather | solution.py:167
  82.4 66.5 %all-gather.12.cloned.1.call-start = ((), (), s32[]{:S(2)}) async-start(), calls=%async_computation.9 | async-start | bytes 3342336 | tf_op jit(solution)/shard_map/all_gather | solution.py:133
  83.2 104.2 %all-gather.14.cloned.1.call-start = ((), (), s32[]{:S(2)}) async-start(), calls=%async_computation.10 | async-start | bytes 1114112 | tf_op jit(solution)/shard_map/all_gather | solution.py:135
  83.9 125.9 %reduce-scatter.11.cloned.1.call-start = ((), (), s32[]{:S(2)}) async-start(), calls=%async_computation.11 | async-start | bytes 1572864 | tf_op jit(solution)/shard_map/reduce_scatter | solution.py:178
  155.8 3.7 copy-start.6
  158.2 3.3 copy-start
  162.9 28.0 %copy-start.14 = (bf16[8,64,512]{2,1,0:T(8,128)(2,1)}, bf16[8,64,512]{2,1,0:T(8,128)(2,1)S(1)}, u32[]{:S(2)}) copy-start(bf16[8,64,512]{2,1,0:T(8,128)(2,1)S(1)} %convolution_convert_fusion.6) | copy-start | bytes 1572868
  162.9 46.9 %copy-start.1 = (f32[256,1024]{1,0:T(8,128)S(1)}, f32[256,1024]{1,0:T(8,128)}, u32[]{:S(2)}) copy-start(f32[256,1024]{1,0:T(8,128)} %param.15) | copy-start | bytes 3145732
  190.3 22.2 %copy-start.12 = (f32[256,1024]{1,0:T(8,128)S(1)}, f32[256,1024]{1,0:T(8,128)}, u32[]{:S(2)}) copy-start(f32[256,1024]{1,0:T(8,128)} %param.29) | copy-start | bytes 3145732
  190.3 23.9 %copy-start.16 = (bf16[128]{0:T(256)(128)(2,1)S(1)}, bf16[128]{0:T(256)(128)(2,1)}, u32[]{:S(2)}) copy-start(bf16[128]{0:T(256)(128)(2,1)} %param.26) | copy-start | bytes 772
  190.3 72.0 %all-gather.18.cloned.1.call-start = ((), (), s32[]{:S(2)}) async-start(), calls=%async_computation.13 | async-start | bytes 4456448 | tf_op jit(solution)/shard_map/all_gather | solution.py:139
  190.9 93.2 %all-gather.16.cloned.1.call-start = ((), (), s32[]{:S(2)}) async-start(), calls=%async_computation.12 | async-start | bytes 1572864 | tf_op jit(solution)/shard_map/all_gather | solution.py:186
  212.4 95.1 %all-gather.20.cloned.1.call-start = ((), (), s32[]{:S(2)}) async-start(), calls=%async_computation.15 | async-start | bytes 1572864 | tf_op jit(solution)/shard_map/all_gather | solution.py:211
  213.4 146.7 %all-gather.22.cloned.1.call-start = ((), (), s32[]{:S(2)}) async-start(), calls=%async_computation.16 | async-start | bytes 4456448 | tf_op jit(solution)/shard_map/all_gather | solution.py:208
  214.2 181.5 %reduce-scatter.15.cloned.1.call-start = ((), (), s32[]{:S(2)}) async-start(), calls=%async_computation.17 | async-start | bytes 1572864 | tf_op jit(solution)/shard_map/reduce_scatter | solution.py:217
  360.1 9.7 %copy-start.17 = (bf16[1024,2048]{1,0:T(8,128)(2,1)S(1)}, bf16[1024,2048]{1,0:T(8,128)(2,1)}, u32[]{:S(2)}) copy-start(bf16[1024,2048]{1,0:T(8,128)(2,1)} %all-gather.18.cloned.1.call-done) | copy-start | bytes 12582916
  368.5 1.3 copy-start.21
  369.8 3.4 copy-start.3
  373.2 54.3 %all-gather.24.cloned.1.call-start = ((), (), s32[]{:S(2)}) async-start(), calls=%async_computation.18 | async-start | bytes 1572864 | tf_op jit(solution)/shard_map/all_gather | solution.py:228
  373.3 5.6 collective-permute-start
  378.9 16.3 %copy-start.10 = (bf16[64,2048]{1,0:T(8,128)(2,1)}, bf16[64,2048]{1,0:T(8,128)(2,1)S(1)}, u32[]{:S(2)}) copy-start(bf16[64,2048]{1,0:T(8,128)(2,1)S(1)} %collective-permute-done) | copy-start | bytes 786436
  378.9 14.3 %collective-permute-start.1 = (bf16[128,2048]{1,0:T(8,128)(2,1)S(1)}, bf16[128,2048]{1,0:T(8,128)(2,1)S(1)}, u32[]{:S(2)}, u32[]{:S(2)}) collective-permute-start(bf16[128,2048]{1,0:T(8,128)(2,1)S(1)} %pad_maximum_fusion.3), channel_id=1, source_target_pairs={{0,28},{2,30},{4,0},{6,2},{8,4},{10,6},{12,8},{14,10},{16,12},{18,... | collective-permute-start | bytes 1572872 | tf_op jit(solution)/shard_map/ppermute | solution.py:18
  393.3 0.8 copy-start.8
  395.2 25.0 %collective-permute-start.2 = (bf16[256,2048]{1,0:T(8,128)(2,1)}, bf16[256,2048]{1,0:T(8,128)(2,1)}, u32[]{:S(2)}, u32[]{:S(2)}) collective-permute-start(bf16[256,2048]{1,0:T(8,128)(2,1)} %pad_maximum_fusion.2), channel_id=1, source_target_pairs={{0,24},{2,26},{4,28},{6,30},{8,0},{10,2},{12,4},{14,6},{16,8},{18,... | collective-permute-start | bytes 3145736 | tf_op jit(solution)/shard_map/ppermute | solution.py:18
  399.9 167.7 %reduce-scatter.21.cloned.1.call-start = ((), (), s32[]{:S(2)}) async-start(), calls=%async_computation.21 | async-start | bytes 1114112 | tf_op jit(solution)/shard_map/reduce_scatter | solution.py:277
  423.2 97.5 %collective-permute-start.3 = (bf16[512,2048]{1,0:T(8,128)(2,1)}, bf16[512,2048]{1,0:T(8,128)(2,1)}, u32[]{:S(2)}, u32[]{:S(2)}) collective-permute-start(bf16[512,2048]{1,0:T(8,128)(2,1)} %pad_maximum_fusion.1), channel_id=1, source_target_pairs={{0,16},{2,18},{4,20},{6,22},{8,24},{10,26},{12,28},{14,30},{16,0},... | collective-permute-start | bytes 6291464 | tf_op jit(solution)/shard_map/ppermute | solution.py:18
  430.6 138.5 %reduce-scatter.17.cloned.1.call-start = ((), (), s32[]{:S(2)}) async-start(), calls=%async_computation.19 | async-start | bytes 1572864 | tf_op jit(solution)/shard_map/reduce_scatter | solution.py:244
  430.8 9.7 %slice-start = ((s8[8388608]{0:T(1024)(128)(4,1)}), s8[4194304]{0:T(1024)(128)(4,1)S(1)}, s32[]{:S(2)}) async-start(s8[8388608]{0:T(1024)(128)(4,1)} %bitcast.77), calls=%async_computation.24 | async-start | bytes 8388608
  433.4 4.9 copy-start.7
  433.4 7.1 slice-start.1
  439.2 2.8 copy-start.4
  440.6 1.4 copy-start.5
  442.0 1.0 copy-start.2
  443.0 2.5 copy-start.18
  443.5 1.2 copy-start.13
  448.4 197.6 %reduce-scatter.13.cloned.1.call-start = ((), (), s32[]{:S(2)}) async-start(), calls=%async_computation.14 | async-start | bytes 1572864 | tf_op jit(solution)/shard_map/reduce_scatter | solution.py:194
  448.4 76.1 %copy-start.11 = (bf16[64,2048]{1,0:T(8,128)(2,1)S(1)}, bf16[64,2048]{1,0:T(8,128)(2,1)}, u32[]{:S(2)}) copy-start(bf16[64,2048]{1,0:T(8,128)(2,1)} %copy-done.10) | copy-start | bytes 786436
  448.4 76.8 %copy-start.9 = (bf16[128,2048]{1,0:T(8,128)(2,1)S(1)}, bf16[128,2048]{1,0:T(8,128)(2,1)}, u32[]{:S(2)}) copy-start(bf16[128,2048]{1,0:T(8,128)(2,1)} %copy-done.8) | copy-start | bytes 1572868
  523.8 7.9 copy-start.20
  537.6 126.4 %reduce-scatter.25.cloned.1.call-start = ((), (), s32[]{:S(2)}) async-start(), calls=%async_computation.23 | async-start | bytes 4456448
  552.2 187.5 %reduce-scatter.23.cloned.1.call-start = ((), (), s32[]{:S(2)}) async-start(), calls=%async_computation.22 | async-start | bytes 4456448 | tf_op jit(solution)/shard_map/reduce_scatter | solution.py:289
  558.5 6.6 copy-start.19
  558.5 250.2 %reduce-scatter.19.cloned.1.call-start = ((), (), s32[]{:S(2)}) async-start(), calls=%async_computation.20 | async-start | bytes 3342336 | tf_op jit(solution)/shard_map/reduce_scatter | solution.py:271
Sparse Core Ops, SparseCore 0:
  82.5 18.5 all-gather.9
  103.4 45.4 all-gather.11
  151.0 36.2 all-gather.13
  190.4 19.3 reduce-scatter.10
  211.8 50.4 all-gather.17
  264.3 19.7 all-gather.15
  286.2 21.2 all-gather.19
  309.7 50.3 all-gather.21
  373.3 18.9 reduce-scatter.14
  400.1 21.8 all-gather.23
  430.7 110.7 reduce-scatter.20
  544.1 19.4 reduce-scatter.16
  566.4 20.7 reduce-scatter.12
  591.0 73.0 reduce-scatter.24
  667.8 71.8 reduce-scatter.22
  743.3 65.3 reduce-scatter.18
